TPU v7x, 512 devices: a whole 4x8x8 slice. The times are simulated.
512 devices in a mesh: aux: 8 (over z), ao: 16 (over y, core), orb: 4 (over x).
Axes of the slice: x: 4, y: 8, z: 8, core: 2. Of those that a mesh axis runs over, the one named last changes fastest.
Arguments:
- integrals: bfloat16 [128, 16, 4, 128, 128], P('aux', 'ao', None, 'orb'), may hold values from -6 to 6
- partner: int32 [16, 4], P('ao'), may hold values from 0 to 15
- pair_count: int32 [16], P('ao'), may hold values from 1 to 4
- occupied_coeff: bfloat16 [2048, 512], P('ao', 'orb'), may hold values from -0.25 to 0.25
- occupied_domain: int32 [16, 4], P('ao', 'orb'), may hold values 0 or 1
- virtual_coeff: bfloat16 [2048, 8192], P('aux', 'ao'), may hold values from -0.125 to 0.125
- virtual_domain: int32 [16, 64], P(None, 'ao'), may hold values 0 or 1
Outputs:
- transformed: bfloat16 [128, 512, 8192], P('aux', 'orb', 'ao')
All inputs are finite; a program needn't handle non-finite values. No bound on the sum of `occupied_domain` or of `virtual_domain` on one device may be relied on, other than what follows from the above.
Results may differ from a plain program's by a relative error of at most 0.0049.
Values may be sent and summed in bfloat16 or wider, within the bound.
A program may use at most 64 MiB of HBM per device.

v0:
```python
import jax
import jax.numpy as jnp
from jax import lax
from jax.sharding import PartitionSpec as P


def local(
    integrals, partner, pair_count, occupied_coeff, occupied_domain, virtual_coeff, virtual_domain
):
    block_size = integrals.shape[4]
    slab_rows = integrals.shape[0]
    slot_count = integrals.shape[2]
    occ_width = occupied_coeff.shape[1]
    occ_local = occupied_coeff * occupied_domain.astype(jnp.bfloat16)
    all_occ = lax.all_gather(occ_local, "ao", axis=0, tiled=True)
    all_ints = lax.all_gather(integrals, "orb", axis=3, tiled=True)
    vir_blocks = virtual_coeff.shape[0] // block_size
    first = lax.axis_index("aux") * vir_blocks
    dom = lax.dynamic_slice_in_dim(virtual_domain, first, vir_blocks, axis=0).astype(jnp.bfloat16)
    dom = jnp.repeat(jnp.repeat(dom, block_size, axis=0), block_size, axis=1)
    vir_masked = lax.all_gather(virtual_coeff * dom, "aux", axis=0, tiled=True)
    picked = all_occ.reshape(-1, block_size, occ_width)[partner[0]]
    slots = jnp.arange(slot_count, dtype=jnp.int32)
    live = (slots < pair_count[0]).astype(jnp.bfloat16)
    picked = picked * live[:, None, None]
    half = jnp.einsum(
        "kri,pkrv->piv", picked, all_ints[:, 0], preferred_element_type=jnp.float32
    ).astype(jnp.bfloat16)
    piece = lax.all_gather(half, "ao", axis=2, tiled=True)
    flat = piece.reshape(slab_rows * occ_width, piece.shape[2])
    product = jnp.dot(flat, vir_masked, preferred_element_type=jnp.float32)
    return product.reshape(slab_rows, occ_width, -1).astype(jnp.bfloat16)


def solution(mesh):
    placed = (
        P("aux", "ao", None, "orb", None),
        P("ao", None),
        P("ao"),
        P("ao", "orb"),
        P("ao", "orb"),
        P("aux", "ao"),
        P(None, "ao"),
    )
    return jax.shard_map(
        local, mesh=mesh, in_specs=placed, out_specs=P("aux", "orb", "ao"), check_vma=False
    )
```

profile of v0, /device:TPU:1, one launch (start us, length us, event | category | flops | bytes accessed | tf_op | source)
XLA Modules:
  0.0 183.8 jit_solution(8361173918025073191)
XLA Ops:
  6.5 0.0 all-gather.4.cloned.1.call-start
  6.5 0.7 all-gather.4.cloned.1.call-update
  7.3 0.0 all-gather.8.cloned.1.call-start
  7.3 0.8 dynamic-slice_convert_fusion
  8.1 0.1 copy.8
  8.2 0.3 broadcast_in_dim.9
  8.5 1.7 bitcast_multiply_fusion
  10.2 0.0 all-gather.8.cloned.1.call-update
  10.3 0.0 all-gather.6.cloned.1.call-start
  11.6 0.7 fusion.19
  12.3 0.8 broadcast_multiply_fusion
  13.0 22.4 %all_gather.12 = bf16[2048,128]{1,0:T(8,128)(2,1)S(1)} all-gather(bf16[128,128]{1,0:T(8,128)(2,1)S(1)} %broadcast_multiply_fusion), channel_id=1, replica_groups=mesh['aux'=8,'ao'=16,'orb'=4] {'ao'}, dimensions={0}, use_global_device_ids=true | all-gather | bytes 557056 | tf_op jit(solution)/shard_map/all_gather | solution.py:15
  35.4 0.6 gather_fusion
  36.0 14.8 %all-gather.4.cloned.1.call-done = bf16[16,1,4,128,128]{4,3,2,1,0:T(8,128)(2,1)} async-done(((bf16[16,1,4,32,128]{4,3,2,1,0:T(8,128)(2,1)}), bf16[16,1,4,128,128]{4,3,2,1,0:T(8,128)(2,1)}) %all-gather.4.cloned.1.call-update) | async-done | bytes 2097168 | tf_op jit(solution)/shard_map/all_gather | solution.py:16
  50.9 2.9 %fusion.13 = bf16[16,128,128]{2,1,0:T(8,128)(2,1)} fusion(bf16[16,1,4,128,128]{4,3,2,1,0:T(8,128)(2,1)} %all-gather.4.cloned.1.call-done, bf16[4,128,128]{2,1,0:T(8,128)(2,1)S(1)} %gather_fusion, bf16[4]{0:T(256)(128)(2,1)S(1)} %compare_convert_fusion), kind=kOutput, calls=%fused_computation.8 | convolution fusion | flops 268959744 | bytes 2752520 | tf_op jit(solution)/shard_map/kri,pkrv->piv/dot_general | solution.py:26
  53.8 0.0 all-gather.6.cloned.1.call-update
  53.8 39.3 %all-gather.8.cloned.1.call-done = bf16[2048,512]{1,0:T(8,128)(2,1)} async-done(((bf16[256,512]{1,0:T(8,128)(2,1)}), bf16[2048,512]{1,0:T(8,128)(2,1)}) %all-gather.8.cloned.1.call-update) | async-done | bytes 2097168 | tf_op jit(solution)/shard_map/all_gather | solution.py:21
  93.1 74.3 %all-gather.6.cloned.1.call-done = bf16[16,128,2048]{2,1,0:T(8,128)(2,1)} async-done(((bf16[16,128,128]{2,1,0:T(8,128)(2,1)}), bf16[16,128,2048]{2,1,0:T(8,128)(2,1)}) %all-gather.6.cloned.1.call-update) | async-done | bytes 8388624 | tf_op jit(solution)/shard_map/all_gather | solution.py:29
  167.4 9.8 %fusion.4 = bf16[16,128,512]{2,1,0:T(8,128)(2,1)} fusion(bf16[16,128,2048]{2,1,0:T(8,128)(2,1)} %all-gather.6.cloned.1.call-done, bf16[2048,512]{1,0:T(8,128)(2,1)} %all-gather.8.cloned.1.call-done), kind=kOutput, calls=%fused_computation.5 | convolution fusion | flops 4296015872 | bytes 12582912 | tf_op jit(solution)/shard_map/dot_general | solution.py:31
  (3 shorter events, 0.0 us)
Async XLA Ops:
  6.5 44.3 %all-gather.4.cloned.1.call-start = ((), (), s32[]{:S(2)}) async-start(), calls=%async_computation | async-start | bytes 2621440 | tf_op jit(solution)/shard_map/all_gather | solution.py:16
  7.3 85.9 %all-gather.8.cloned.1.call-start = ((), (), s32[]{:S(2)}) async-start(), calls=%async_computation.2 | async-start | bytes 2359296 | tf_op jit(solution)/shard_map/all_gather | solution.py:21
  10.3 157.2 %all-gather.6.cloned.1.call-start = ((), (), s32[]{:S(2)}) async-start(), calls=%async_computation.1 | async-start | bytes 8912896 | tf_op jit(solution)/shard_map/all_gather | solution.py:29
Sparse Core Ops, SparseCore 0:
  9.4 41.3 all-gather.3
  52.9 40.1 all-gather.7
  95.2 72.2 all-gather.5
where the time goes:
time: 184 us
  waiting for transfers between devices  129 us (70%)
  blocking collectives  22.4 us (12%)
  between operations  14.4 us (8%)
  matrix products  12.7 us (7%)
  other arithmetic  3.9 us (2%)
    all_gather x1, waiting for transfers between devices, local(): piece = lax.all_gather(half, 'ao', axis=2, tiled=True)  74.3 us
    all_gather x1, waiting for transfers between devices, local(): vir_masked = lax.all_gather(virtual_coeff * dom, 'aux', axis=0, tiled=True)  39.3 us
    all_gather x1, blocking collectives, local(): all_occ = lax.all_gather(occ_local, 'ao', axis=0, tiled=True)  22.4 us
    all_gather x1, waiting for transfers between devices, local(): all_ints = lax.all_gather(integrals, 'orb', axis=3, tiled=True)  14.8 us
    dot_general x1, matrix products, local(): product = jnp.dot(flat, vir_masked, preferred_element_type=jnp.float32)  9.82 us
  transfers between devices with their start and end apart: 3, of which 3 were waited for; matrix products, arithmetic and copies ran while one was open for 4% of the time, Pallas kernels for 0%

commit v1 on v0

--- a/solution.py
+++ b/solution.py
@@ -18,7 +18,17 @@
     first = lax.axis_index("aux") * vir_blocks
     dom = lax.dynamic_slice_in_dim(virtual_domain, first, vir_blocks, axis=0).astype(jnp.bfloat16)
     dom = jnp.repeat(jnp.repeat(dom, block_size, axis=0), block_size, axis=1)
-    vir_masked = lax.all_gather(virtual_coeff * dom, "aux", axis=0, tiled=True)
+    shard = virtual_coeff * dom
+    ways = lax.axis_size("aux")
+    up = [(d, (d + 1) % ways) for d in range(ways)]
+    down = [(d, (d - 1) % ways) for d in range(ways)]
+    earlier, later = ([shard], [shard])
+    for _ in range(ways // 2):
+        earlier.append(lax.ppermute(earlier[-1], "aux", up))
+    for _ in range((ways - 1) // 2):
+        later.append(lax.ppermute(later[-1], "aux", down))
+    line = jnp.concatenate([*earlier[::-1], *later[1:]], axis=0)
+    vir_masked = jnp.roll(line, (lax.axis_index("aux") - ways // 2) * shard.shape[0], axis=0)
     picked = all_occ.reshape(-1, block_size, occ_width)[partner[0]]
     slots = jnp.arange(slot_count, dtype=jnp.int32)
     live = (slots < pair_count[0]).astype(jnp.bfloat16)

time: 184 us -> 141 us (0.77)
  waiting for transfers between devices: 129 us -> 53.8 us
  starting transfers between devices: 0.08 us -> 22.8 us
  local copies, waits for them, and re-layouts: 1.02 us -> 12.7 us
  other arithmetic: 3.9 us -> 1.56 us
    all_gather x1, waiting for transfers between devices: 74.3 us -> 19.5 us  [local(): piece = lax.all_gather(half, 'ao', axis=2, tiled=True)]
    all_gather x1 -> x0, waiting for transfers between devices: 39.3 us -> none  [local(): vir_masked = lax.all_gather(virtual_coeff * dom, 'aux', axis=0, tiled=True)]
    ppermute x0 -> x7, starting transfers between devices: none -> 22.7 us  [the longest x3 13.7 us: local(): later.append(lax.ppermute(later[-1], 'aux', down))]
    ppermute x0 -> x7, waiting for transfers between devices: none -> 15.6 us  [the longest x4 15.6 us: local(): earlier.append(lax.ppermute(earlier[-1], 'aux', up))]
    unnamed x0 -> x19, local copies, waits for them, and re-layouts: none -> 11 us
    all_gather x1, waiting for transfers between devices: 14.8 us -> 17.9 us  [local(): all_ints = lax.all_gather(integrals, 'orb', axis=3, tiled=True)]
  transfers between devices with their start and end apart: 3 -> 9, of which waited for: 3 -> 6; matrix products, arithmetic and copies ran while one was open for 4% -> 10% of each run, Pallas kernels for 0% -> 0%
where the time goes in v1:
time: 141 us
  waiting for transfers between devices  53.8 us (38%)
  starting transfers between devices  22.8 us (16%)
  blocking collectives  22.4 us (16%)
  between operations  14.9 us (11%)
  matrix products  12.8 us (9%)
  local copies, waits for them, and re-layouts  12.7 us (9%)
  other arithmetic  1.56 us (1%)
    all_gather x1, blocking collectives, local(): all_occ = lax.all_gather(occ_local, 'ao', axis=0, tiled=True)  22.4 us
    all_gather x1, waiting for transfers between devices, local(): piece = lax.all_gather(half, 'ao', axis=2, tiled=True)  19.5 us
    all_gather x1, waiting for transfers between devices, local(): all_ints = lax.all_gather(integrals, 'orb', axis=3, tiled=True)  17.9 us
    ppermute x4, waiting for transfers between devices, local(): earlier.append(lax.ppermute(earlier[-1], 'aux', up))  15.6 us
    ppermute x3, starting transfers between devices, local(): later.append(lax.ppermute(later[-1], 'aux', down))  13.7 us
    unnamed x19, local copies, waits for them, and re-layouts  11 us
    dot_general x1, matrix products, local(): product = jnp.dot(flat, vir_masked, preferred_element_type=jnp.float32)  9.82 us
    ppermute x4, starting transfers between devices, local(): earlier.append(lax.ppermute(earlier[-1], 'aux', up))  9 us
  transfers between devices with their start and end apart: 9, of which 6 were waited for; matrix products, arithmetic and copies ran while one was open for 10% of the time, Pallas kernels for 0%

profile of v1, /device:TPU:1, one launch (start us, length us, event | category | flops | bytes accessed | tf_op | source)
XLA Modules:
  0.0 140.8 jit_solution(7916766153099443837)
XLA Ops:
  9.3 0.8 broadcast_multiply_fusion
  10.0 22.4 %all_gather.9 = bf16[2048,128]{1,0:T(8,128)(2,1)S(1)} all-gather(bf16[128,128]{1,0:T(8,128)(2,1)S(1)} %broadcast_multiply_fusion), channel_id=1, replica_groups=mesh['aux'=8,'ao'=16,'orb'=4] {'ao'}, dimensions={0}, use_global_device_ids=true | all-gather | bytes 557056 | tf_op jit(solution)/shard_map/all_gather | solution.py:15
  33.0 17.9 %all-gather.3.cloned.1.call-done = bf16[16,1,4,128,128]{4,3,2,1,0:T(8,128)(2,1)} async-done(((bf16[16,1,4,32,128]{4,3,2,1,0:T(8,128)(2,1)}), bf16[16,1,4,128,128]{4,3,2,1,0:T(8,128)(2,1)}) %all-gather.3.cloned.1.call-update) | async-done | bytes 2097168 | tf_op jit(solution)/shard_map/all_gather | solution.py:16
  50.9 2.9 %fusion.14 = bf16[16,128,128]{2,1,0:T(8,128)(2,1)} fusion(bf16[16,1,4,128,128]{4,3,2,1,0:T(8,128)(2,1)} %all-gather.3.cloned.1.call-done, bf16[4,128,128]{2,1,0:T(8,128)(2,1)S(1)} %gather_fusion, bf16[4]{0:T(256)(128)(2,1)S(1)} %compare_convert_fusion), kind=kOutput, calls=%fused_computation.9 | convolution fusion | flops 268959744 | bytes 2752520 | tf_op jit(solution)/shard_map/kri,pkrv->piv/dot_general | solution.py:36
  54.4 3.3 %collective-permute-start = (bf16[256,512]{1,0:T(8,128)(2,1)S(1)}, bf16[256,512]{1,0:T(8,128)(2,1)S(1)}, u32[]{:S(2)}, u32[]{:S(2)}) collective-permute-start(bf16[256,512]{1,0:T(8,128)(2,1)S(1)} %bitcast_multiply_fusion), channel_id=1, source_target_pairs={{0,64},{64,128},{128,192},{192,256},{256,320},{320,384},{384,448},... | collective-permute-start | bytes 786440 | tf_op jit(solution)/shard_map/ppermute | solution.py:27
  57.7 8.1 %collective-permute-done = bf16[256,512]{1,0:T(8,128)(2,1)S(1)} collective-permute-done((bf16[256,512]{1,0:T(8,128)(2,1)S(1)}, bf16[256,512]{1,0:T(8,128)(2,1)S(1)}, u32[]{:S(2)}, u32[]{:S(2)}) %collective-permute-start) | collective-permute-done | bytes 262176 | tf_op jit(solution)/shard_map/ppermute | solution.py:27
  65.9 1.9 %collective-permute-start.1 = (bf16[256,512]{1,0:T(8,128)(2,1)S(1)}, bf16[256,512]{1,0:T(8,128)(2,1)S(1)}, u32[]{:S(2)}, u32[]{:S(2)}) collective-permute-start(bf16[256,512]{1,0:T(8,128)(2,1)S(1)} %collective-permute-done), channel_id=1, source_target_pairs={{0,64},{64,128},{128,192},{192,256},{256,320},{320,384},{384,448},... | collective-permute-start | bytes 786440 | tf_op jit(solution)/shard_map/ppermute | solution.py:27
  67.8 4.6 %collective-permute-start.4 = (bf16[256,512]{1,0:T(8,128)(2,1)S(1)}, bf16[256,512]{1,0:T(8,128)(2,1)S(1)}, u32[]{:S(2)}, u32[]{:S(2)}) collective-permute-start(bf16[256,512]{1,0:T(8,128)(2,1)S(1)} %bitcast_multiply_fusion), channel_id=1, source_target_pairs={{0,448},{64,0},{128,64},{192,128},{256,192},{320,256},{384,320},{4... | collective-permute-start | bytes 786440 | tf_op jit(solution)/shard_map/ppermute | solution.py:29
  72.4 3.2 %collective-permute-done.1 = bf16[256,512]{1,0:T(8,128)(2,1)S(1)} collective-permute-done((bf16[256,512]{1,0:T(8,128)(2,1)S(1)}, bf16[256,512]{1,0:T(8,128)(2,1)S(1)}, u32[]{:S(2)}, u32[]{:S(2)}) %collective-permute-start.1) | collective-permute-done | bytes 262176 | tf_op jit(solution)/shard_map/ppermute | solution.py:27
  75.5 1.9 %collective-permute-start.2 = (bf16[256,512]{1,0:T(8,128)(2,1)S(1)}, bf16[256,512]{1,0:T(8,128)(2,1)S(1)}, u32[]{:S(2)}, u32[]{:S(2)}) collective-permute-start(bf16[256,512]{1,0:T(8,128)(2,1)S(1)} %collective-permute-done.1), channel_id=1, source_target_pairs={{0,64},{64,128},{128,192},{192,256},{256,320},{320,384},{384,448},... | collective-permute-start | bytes 786440 | tf_op jit(solution)/shard_map/ppermute | solution.py:27
  77.4 4.6 %collective-permute-start.5 = (bf16[256,512]{1,0:T(8,128)(2,1)S(1)}, bf16[256,512]{1,0:T(8,128)(2,1)S(1)}, u32[]{:S(2)}, u32[]{:S(2)}) collective-permute-start(bf16[256,512]{1,0:T(8,128)(2,1)S(1)} %collective-permute-done.4), channel_id=1, source_target_pairs={{0,448},{64,0},{128,64},{192,128},{256,192},{320,256},{384,320},{4... | collective-permute-start | bytes 786440 | tf_op jit(solution)/shard_map/ppermute | solution.py:29
  82.0 2.4 %collective-permute-done.2 = bf16[256,512]{1,0:T(8,128)(2,1)S(1)} collective-permute-done((bf16[256,512]{1,0:T(8,128)(2,1)S(1)}, bf16[256,512]{1,0:T(8,128)(2,1)S(1)}, u32[]{:S(2)}, u32[]{:S(2)}) %collective-permute-start.2) | collective-permute-done | bytes 262176 | tf_op jit(solution)/shard_map/ppermute | solution.py:27
  84.4 1.9 %collective-permute-start.3 = (bf16[256,512]{1,0:T(8,128)(2,1)S(1)}, bf16[256,512]{1,0:T(8,128)(2,1)S(1)}, u32[]{:S(2)}, u32[]{:S(2)}) collective-permute-start(bf16[256,512]{1,0:T(8,128)(2,1)S(1)} %collective-permute-done.2), channel_id=1, source_target_pairs={{0,64},{64,128},{128,192},{192,256},{256,320},{320,384},{384,448},... | collective-permute-start | bytes 786440 | tf_op jit(solution)/shard_map/ppermute | solution.py:27
  86.4 4.6 %collective-permute-start.6 = (bf16[256,512]{1,0:T(8,128)(2,1)S(1)}, bf16[256,512]{1,0:T(8,128)(2,1)S(1)}, u32[]{:S(2)}, u32[]{:S(2)}) collective-permute-start(bf16[256,512]{1,0:T(8,128)(2,1)S(1)} %collective-permute-done.5), channel_id=1, source_target_pairs={{0,448},{64,0},{128,64},{192,128},{256,192},{320,256},{384,320},{4... | collective-permute-start | bytes 786440 | tf_op jit(solution)/shard_map/ppermute | solution.py:29
  90.9 2.0 %collective-permute-done.3 = bf16[256,512]{1,0:T(8,128)(2,1)S(1)} collective-permute-done((bf16[256,512]{1,0:T(8,128)(2,1)S(1)}, bf16[256,512]{1,0:T(8,128)(2,1)S(1)}, u32[]{:S(2)}, u32[]{:S(2)}) %collective-permute-start.3) | collective-permute-done | bytes 262176 | tf_op jit(solution)/shard_map/ppermute | solution.py:27
  92.9 0.7 constant_dynamic-update-slice_fusion.15
  93.6 0.7 constant_dynamic-update-slice_fusion.14
  94.4 0.8 constant_dynamic-update-slice_fusion.13
  97.3 0.7 constant_dynamic-update-slice_fusion.9
  98.8 0.7 constant_dynamic-update-slice_fusion.7
  99.5 0.7 constant_dynamic-update-slice_fusion.6
  103.1 0.7 constant_dynamic-update-slice_fusion.1
  104.6 19.5 %all-gather.5.cloned.1.call-done = bf16[16,128,2048]{2,1,0:T(8,128)(2,1)} async-done(((bf16[16,128,128]{2,1,0:T(8,128)(2,1)}), bf16[16,128,2048]{2,1,0:T(8,128)(2,1)}) %all-gather.5.cloned.1.call-update) | async-done | bytes 8388624 | tf_op jit(solution)/shard_map/all_gather | solution.py:39
  124.1 9.8 %fusion.5 = bf16[16,128,512]{2,1,0:T(8,128)(2,1)} fusion(bf16[16,128,2048]{2,1,0:T(8,128)(2,1)} %all-gather.5.cloned.1.call-done, bf16[4096,512]{1,0:T(8,128)(2,1)} %constant_dynamic-update-slice_fusion, s32[]{:T(128)S(6)} %select_n.29), kind=kOutput, calls=%fused_computation.6 | convolution fusion | flops 4296015872 | bytes 12582916 | tf_op jit(solution)/shard_map/dot_general | solution.py:41
  (29 shorter events, 9.1 us)
Async XLA Ops:
  6.5 47.3 %copy-start.1 = (s32[16,4]{0,1:T(4,128)S(1)}, s32[16,4]{0,1:T(4,128)}, u32[]{:S(2)}) copy-start(s32[16,4]{0,1:T(4,128)} %param.13) | copy-start | bytes 772
  6.5 47.9 %copy-start = (bf16[256,512]{1,0:T(8,128)(2,1)S(1)}, bf16[256,512]{1,0:T(8,128)(2,1)}, u32[]{:S(2)}) copy-start(bf16[256,512]{1,0:T(8,128)(2,1)} %param.12) | copy-start | bytes 786436
  6.5 44.3 %all-gather.3.cloned.1.call-start = ((), (), s32[]{:S(2)}) async-start(), calls=%async_computation | async-start | bytes 2621440 | tf_op jit(solution)/shard_map/all_gather | solution.py:16
  7.3 116.9 %all-gather.5.cloned.1.call-start = ((), (), s32[]{:S(2)}) async-start(), calls=%async_computation.1 | async-start | bytes 8912896 | tf_op jit(solution)/shard_map/all_gather | solution.py:39
  54.4 11.4 %collective-permute-start = (bf16[256,512]{1,0:T(8,128)(2,1)S(1)}, bf16[256,512]{1,0:T(8,128)(2,1)S(1)}, u32[]{:S(2)}, u32[]{:S(2)}) collective-permute-start(bf16[256,512]{1,0:T(8,128)(2,1)S(1)} %bitcast_multiply_fusion), channel_id=1, source_target_pairs={{0,64},{64,128},{128,192},{192,256},{256,320},{320,384},{384,448},... | collective-permute-start | bytes 786440 | tf_op jit(solution)/shard_map/ppermute | solution.py:27
  65.9 9.6 %collective-permute-start.1 = (bf16[256,512]{1,0:T(8,128)(2,1)S(1)}, bf16[256,512]{1,0:T(8,128)(2,1)S(1)}, u32[]{:S(2)}, u32[]{:S(2)}) collective-permute-start(bf16[256,512]{1,0:T(8,128)(2,1)S(1)} %collective-permute-done), channel_id=1, source_target_pairs={{0,64},{64,128},{128,192},{192,256},{256,320},{320,384},{384,448},... | collective-permute-start | bytes 786440 | tf_op jit(solution)/shard_map/ppermute | solution.py:27
  67.8 9.7 %collective-permute-start.4 = (bf16[256,512]{1,0:T(8,128)(2,1)S(1)}, bf16[256,512]{1,0:T(8,128)(2,1)S(1)}, u32[]{:S(2)}, u32[]{:S(2)}) collective-permute-start(bf16[256,512]{1,0:T(8,128)(2,1)S(1)} %bitcast_multiply_fusion), channel_id=1, source_target_pairs={{0,448},{64,0},{128,64},{192,128},{256,192},{320,256},{384,320},{4... | collective-permute-start | bytes 786440 | tf_op jit(solution)/shard_map/ppermute | solution.py:29
  75.5 8.9 %collective-permute-start.2 = (bf16[256,512]{1,0:T(8,128)(2,1)S(1)}, bf16[256,512]{1,0:T(8,128)(2,1)S(1)}, u32[]{:S(2)}, u32[]{:S(2)}) collective-permute-start(bf16[256,512]{1,0:T(8,128)(2,1)S(1)} %collective-permute-done.1), channel_id=1, source_target_pairs={{0,64},{64,128},{128,192},{192,256},{256,320},{320,384},{384,448},... | collective-permute-start | bytes 786440 | tf_op jit(solution)/shard_map/ppermute | solution.py:27
  77.4 8.9 %collective-permute-start.5 = (bf16[256,512]{1,0:T(8,128)(2,1)S(1)}, bf16[256,512]{1,0:T(8,128)(2,1)S(1)}, u32[]{:S(2)}, u32[]{:S(2)}) collective-permute-start(bf16[256,512]{1,0:T(8,128)(2,1)S(1)} %collective-permute-done.4), channel_id=1, source_target_pairs={{0,448},{64,0},{128,64},{192,128},{256,192},{320,256},{384,320},{4... | collective-permute-start | bytes 786440 | tf_op jit(solution)/shard_map/ppermute | solution.py:29
  84.4 8.5 %collective-permute-start.3 = (bf16[256,512]{1,0:T(8,128)(2,1)S(1)}, bf16[256,512]{1,0:T(8,128)(2,1)S(1)}, u32[]{:S(2)}, u32[]{:S(2)}) collective-permute-start(bf16[256,512]{1,0:T(8,128)(2,1)S(1)} %collective-permute-done.2), channel_id=1, source_target_pairs={{0,64},{64,128},{128,192},{192,256},{256,320},{320,384},{384,448},... | collective-permute-start | bytes 786440 | tf_op jit(solution)/shard_map/ppermute | solution.py:27
  86.4 11.7 %collective-permute-start.6 = (bf16[256,512]{1,0:T(8,128)(2,1)S(1)}, bf16[256,512]{1,0:T(8,128)(2,1)S(1)}, u32[]{:S(2)}, u32[]{:S(2)}) collective-permute-start(bf16[256,512]{1,0:T(8,128)(2,1)S(1)} %collective-permute-done.5), channel_id=1, source_target_pairs={{0,448},{64,0},{128,64},{192,128},{256,192},{320,256},{384,320},{4... | collective-permute-start | bytes 786440 | tf_op jit(solution)/shard_map/ppermute | solution.py:29
Sparse Core Ops, SparseCore 0:
  9.4 41.3 all-gather.2
  54.0 70.1 all-gather.4
